TPU v7x, 256 devices: a whole 4x4x8 slice. The times are simulated.
256 devices in a mesh: section: 8 (over z_hi, core), fsdp: 4 (over x), tensor: 8 (over y, z_lo).
Axes of the slice: x: 4, y: 4, z: 8 (z_hi: 4, z_lo: 2; z = z_hi * 2 + z_lo), core: 2. Of those that a mesh axis runs over, the one named last changes fastest.
Arguments:
- hidden: bfloat16 [8, 512, 8192], P('section', 'fsdp', 'tensor'), may hold values from -16 to 16
- encoder_weight: bfloat16 [8, 1024, 8192], P('section', 'fsdp', 'tensor'), may hold values from -0.0625 to 0.0625
- decoder_weight: bfloat16 [8, 1024, 8192], P('section', 'fsdp', 'tensor'), may hold values from -16 to 16
- query_weight: bfloat16 [8, 8192, 8192], P('section', 'fsdp', 'tensor'), may hold values from -32 to 32
- key_weight: bfloat16 [8, 8192, 1024], P('section', 'fsdp', 'tensor'), may hold values from -1 to 1
- value_weight: bfloat16 [8, 8192, 1024], P('section', 'fsdp', 'tensor'), may hold values from -0.0625 to 0.0625
- segments: int32 [8, 4, 128], P('section', 'fsdp'), may hold values from 0 to 3, never falling along the last dimension, each value on 1 to 64 neighbouring positions
- out_grad: bfloat16 [8, 512, 8192], P('section', 'fsdp', 'tensor'), may hold values from -6 to 6
Outputs:
- attention: bfloat16 [8, 512, 8192], P('section', 'fsdp', 'tensor')
- hidden_grad: bfloat16 [8, 512, 8192], P('section', 'fsdp', 'tensor')
- encoder_grad: float32 [8, 1024, 8192], P('section', 'fsdp', 'tensor')
- decoder_grad: float32 [8, 1024, 8192], P('section', 'fsdp', 'tensor')
Inputs may be any that keep to these rules, and one draw needn't show every extreme that they name: `segments`: segment ids never fall along a row, and attention stays inside one document of one row; each document spans at most 64 tokens, and some document spans exactly that many.
All inputs are finite; a program needn't handle non-finite values.
Results may differ from a plain program's by a relative error of at most 0.025.
Values may be sent and summed in bfloat16 or wider, within the bound.
No kernel may reach another device: no remote copies, remote signals or barrier semaphores. Data moves between devices by JAX's collectives and lax.ppermute only.
A program may use at most 128 MiB of HBM per device.

v0:
```python
import math
import jax
import jax.numpy as jnp
from jax import lax
from jax.sharding import PartitionSpec as P

D = 8192
DH = 128
NORM_EPS = 1e-05
ROPE_BASE = 500000.0
NEG_FILL = -1e30


def passed_along(value, axis, steps):
    count = lax.axis_size(axis)
    pairs = [(source, (source + steps) % count) for source in range(count)]
    return lax.ppermute(value, axis, pairs)


def rope_tables(segment_row, dim):
    length = segment_row.shape[0]
    positions = jnp.arange(length, dtype=jnp.int32)
    earlier = jnp.sum((segment_row[None, :] < segment_row[:, None]).astype(jnp.int32), axis=1)
    places = (positions - earlier).astype(jnp.float32)
    frequency = jnp.exp(jnp.arange(0, dim, 2).astype(jnp.float32) * (-math.log(ROPE_BASE) / dim))
    angles = places[:, None] * frequency[None, :]
    allowed = (segment_row[None, :] == segment_row[:, None]) & (
        positions[None, :] <= positions[:, None]
    )
    return (jnp.cos(angles), jnp.sin(angles), allowed)


def rotate(values, cosine, sine):
    half_dim = values.shape[-1] // 2
    first_half = values[..., :half_dim]
    second_half = values[..., half_dim:]
    cosine_rows = cosine[:, None, :]
    sine_rows = sine[:, None, :]
    return jnp.concatenate(
        [
            first_half * cosine_rows - second_half * sine_rows,
            second_half * cosine_rows + first_half * sine_rows,
        ],
        axis=-1,
    )


def unrotate(grads, cosine, sine):
    half_dim = grads.shape[-1] // 2
    first_half = grads[..., :half_dim]
    second_half = grads[..., half_dim:]
    cosine_rows = cosine[:, None, :]
    sine_rows = sine[:, None, :]
    return jnp.concatenate(
        [
            first_half * cosine_rows + second_half * sine_rows,
            second_half * cosine_rows - first_half * sine_rows,
        ],
        axis=-1,
    )


def product(form, left, right):
    return jnp.einsum(form, left, right, preferred_element_type=jnp.float32)


def attend(queries, keys_in, values_in, upstream, segment_row, head_count, pair_count):
    length = queries.shape[0]
    group_size = head_count // pair_count
    cosine, sine, allowed = rope_tables(segment_row, DH)
    query_rot = (
        rotate(queries.reshape(length, head_count, DH), cosine, sine)
        .astype(jnp.bfloat16)
        .reshape(length, pair_count, group_size, DH)
    )
    key_rot = rotate(keys_in.reshape(length, pair_count, DH), cosine, sine).astype(jnp.bfloat16)
    value_heads = values_in.reshape(length, pair_count, DH).astype(jnp.bfloat16)
    factor = 1.0 / math.sqrt(DH)
    scores = product("tkgd,skd->kgts", query_rot, key_rot) * factor
    scores = jnp.where(allowed, scores, NEG_FILL)
    row_max = jnp.max(scores, axis=-1, keepdims=True)
    exponent = jnp.exp(scores - row_max)
    probs = exponent / jnp.sum(exponent, axis=-1, keepdims=True)
    probs_low = probs.astype(jnp.bfloat16)
    mixed = product("kgts,skd->tkgd", probs_low, value_heads).reshape(length, head_count * DH)
    cot_heads = upstream.reshape(length, pair_count, group_size, DH)
    prob_grad = product("tkgd,skd->kgts", cot_heads, value_heads)
    value_grad = product("kgts,tkgd->skd", probs_low, cot_heads)
    score_grad = probs * (prob_grad - jnp.sum(probs * prob_grad, axis=-1, keepdims=True))
    score_grad_low = score_grad.astype(jnp.bfloat16)
    query_grad = product("kgts,skd->tkgd", score_grad_low, key_rot) * factor
    key_grad = product("kgts,tkgd->skd", score_grad_low, query_rot) * factor
    query_grad = unrotate(query_grad.reshape(length, head_count, DH), cosine, sine).reshape(
        length, head_count * DH
    )
    key_grad = unrotate(key_grad, cosine, sine).reshape(length, pair_count * DH)
    return (
        mixed.astype(jnp.bfloat16),
        query_grad.astype(jnp.bfloat16),
        key_grad.astype(jnp.bfloat16),
        value_grad.reshape(length, pair_count * DH).astype(jnp.bfloat16),
    )


def row_total(values):
    return lax.psum(values, "tensor")


def token_sum(left, right):
    return lax.psum_scatter(
        lax.dot_general(
            left, right, (((0,), (0,)), ((), ())), preferred_element_type=jnp.float32
        ).astype(jnp.bfloat16),
        "fsdp",
        scatter_dimension=0,
        tiled=True,
    ).astype(jnp.float32)


def body(
    hidden,
    encoder_weight,
    decoder_weight,
    query_weight,
    key_weight,
    value_weight,
    segments,
    out_grad,
):
    residual = hidden[0]
    segment_row = segments[0, 0]
    upstream = out_grad[0]
    contract_last = (((1,), (1,)), ((), ()))
    encoder_rows, decoder_rows = (
        lax.all_gather(encoder_weight[0], "fsdp", axis=0, tiled=True),
        lax.all_gather(decoder_weight[0], "fsdp", axis=0, tiled=True),
    )
    code_partial = lax.dot_general(
        residual, encoder_rows, contract_last, preferred_element_type=jnp.float32
    )
    code_sent = lax.psum(code_partial, "tensor").astype(jnp.bfloat16)
    code_received = passed_along(code_sent, "section", 1)
    decoded = jnp.dot(code_received, decoder_rows, preferred_element_type=jnp.float32)
    norm_factor = lax.rsqrt(row_total(jnp.sum(decoded * decoded, axis=1)) / D + NORM_EPS)[:, None]
    normed = (decoded * norm_factor).astype(jnp.bfloat16)
    normed_full = lax.all_gather(normed, "tensor", axis=1, tiled=True)
    query_width = query_weight.shape[2]
    key_width = key_weight.shape[2]
    query_rows, key_rows, value_rows = (
        lax.all_gather(query_weight[0], "fsdp", axis=0, tiled=True),
        lax.all_gather(key_weight[0], "fsdp", axis=0, tiled=True),
        lax.all_gather(value_weight[0], "fsdp", axis=0, tiled=True),
    )
    queries = jnp.dot(normed_full, query_rows, preferred_element_type=jnp.float32)
    keys_all = jnp.dot(normed_full, key_rows, preferred_element_type=jnp.float32)
    values_all = jnp.dot(normed_full, value_rows, preferred_element_type=jnp.float32)
    mixed, query_grad, key_grad, value_grad = attend(
        queries, keys_all, values_all, upstream, segment_row, query_width // DH, key_width // DH
    )
    total = lax.dot_general(
        query_rows, query_grad, contract_last, preferred_element_type=jnp.float32
    )
    total = total + lax.dot_general(
        key_rows, key_grad, contract_last, preferred_element_type=jnp.float32
    )
    total = total + lax.dot_general(
        value_rows, value_grad, contract_last, preferred_element_type=jnp.float32
    )
    normed_grad = (
        lax.psum_scatter(total.astype(jnp.bfloat16), "tensor", scatter_dimension=0, tiled=True)
        .astype(jnp.float32)
        .T
    )
    inner_dot = row_total(jnp.sum(normed_grad * decoded, axis=1))[:, None]
    decoded_grad = (norm_factor * normed_grad - decoded * norm_factor**3 * inner_dot / D).astype(
        jnp.bfloat16
    )
    decoder_grad = token_sum(code_received, decoded_grad)
    code_grad_partial = lax.dot_general(
        decoded_grad, decoder_rows, contract_last, preferred_element_type=jnp.float32
    )
    code_grad_sent = lax.psum(code_grad_partial.astype(jnp.bfloat16), "tensor")
    code_grad = passed_along(code_grad_sent, "section", -1)
    encoder_grad = token_sum(code_grad, residual)
    hidden_grad = jnp.dot(code_grad, encoder_rows, preferred_element_type=jnp.float32).astype(
        jnp.bfloat16
    )
    return (mixed[None], hidden_grad[None], encoder_grad[None], decoder_grad[None])


def solution(mesh):
    placed = (
        P("section", "fsdp", "tensor"),
        P("section", "fsdp", "tensor"),
        P("section", "fsdp", "tensor"),
        P("section", "fsdp", "tensor"),
        P("section", "fsdp", "tensor"),
        P("section", "fsdp", "tensor"),
        P("section", "fsdp", None),
        P("section", "fsdp", "tensor"),
    )
    return jax.shard_map(
        body,
        mesh=mesh,
        in_specs=placed,
        out_specs=(
            P("section", "fsdp", "tensor"),
            P("section", "fsdp", "tensor"),
            P("section", "fsdp", "tensor"),
            P("section", "fsdp", "tensor"),
        ),
        check_vma=False,
    )
```

profile of v0, /device:TPU:1, one launch (start us, length us, event | category | flops | bytes accessed | tf_op | source)
XLA Modules:
  0.0 637.2 jit_solution(18349268483296418803)
XLA Ops:
  9.4 37.3 %all-gather.14.cloned.1.call-done = bf16[1,1024,1024]{2,1,0:T(8,128)(2,1)} async-done(((bf16[1,256,1024]{2,1,0:T(8,128)(2,1)}), bf16[1,1024,1024]{2,1,0:T(8,128)(2,1)}) %all-gather.14.cloned.1.call-update) | async-done | bytes 2097168 | tf_op jit(solution)/shard_map/all_gather | solution.py:135
  46.8 2.4 fusion.18
  49.2 38.5 %all-reduce.4 = bf16[128,1024]{1,0:T(8,128)(2,1)S(1)} all-reduce(f32[128,1024]{1,0:T(8,128)S(1)} %fusion.18), channel_id=1, replica_groups=mesh['section'=8,'fsdp'=4,'tensor'=8] {'tensor'}, use_global_device_ids=true, to_apply=%region_0.0 | all-reduce | flops 131072 | bytes 786432 | tf_op jit(solution)/shard_map/psum | solution.py:141
  87.7 8.9 %collective-permute-start = (bf16[128,1024]{1,0:T(8,128)(2,1)S(1)}, bf16[128,1024]{1,0:T(8,128)(2,1)S(1)}, u32[]{:S(2)}, u32[]{:S(2)}) collective-permute-start(bf16[128,1024]{1,0:T(8,128)(2,1)S(1)} %all-reduce.4), channel_id=1, source_target_pairs={{0,32},{32,64},{64,96},{96,128},{128,160},{160,192},{192,224},{224... | collective-permute-start | bytes 786440 | tf_op jit(solution)/shard_map/ppermute | solution.py:17
  96.6 4.6 collective-permute-done
  101.2 2.2 multiply_reduce_fusion.1
  103.5 15.4 %psum.29 = f32[128]{0:T(128)S(1)} all-reduce(f32[128]{0:T(128)S(1)} %get-tuple-element.26), channel_id=1, replica_groups=mesh['section'=8,'fsdp'=4,'tensor'=8] {'tensor'}, use_global_device_ids=true, to_apply=%region_2.0 | all-reduce | flops 128 | bytes 1024 | tf_op jit(solution)/shard_map/psum | solution.py:106
  123.7 52.0 %all-gather.12.cloned.1.call-done = bf16[128,8192]{1,0:T(8,128)(2,1)} async-done(((bf16[128,1024]{1,0:T(8,128)(2,1)}), bf16[128,8192]{1,0:T(8,128)(2,1)}) %all-gather.12.cloned.1.call-update) | async-done | bytes 2097168 | tf_op jit(solution)/shard_map/all_gather | solution.py:146
  175.7 3.3 fusion.35
  179.8 30.6 %all-gather.18.cloned.1.call-done = bf16[1,8192,128]{2,1,0:T(8,128)(2,1)} async-done(((bf16[1,2048,128]{2,1,0:T(8,128)(2,1)}), bf16[1,8192,128]{2,1,0:T(8,128)(2,1)}) %all-gather.18.cloned.1.call-update) | async-done | bytes 2097168 | tf_op jit(solution)/shard_map/all_gather | solution.py:152
  210.4 2.9 fusion.44
  213.3 155.4 %all-gather.22.cloned.1.call-done = bf16[1,8192,1024]{2,1,0:T(8,128)(2,1)} async-done(((bf16[1,2048,1024]{2,1,0:T(8,128)(2,1)}), bf16[1,8192,1024]{2,1,0:T(8,128)(2,1)}) %all-gather.22.cloned.1.call-update) | async-done | bytes 16777232 | tf_op jit(solution)/shard_map/all_gather | solution.py:150
  368.7 8.1 %fusion.22 = f32[16,8,8,128]{3,1,2,0:T(8,128)S(1)} fusion(bf16[128,8192]{1,0:T(8,128)(2,1)S(1)} %copy-done.1, bf16[1,8192,1024]{2,1,0:T(8,128)(2,1)} %all-gather.22.cloned.1.call-done), kind=kOutput, calls=%fused_computation.29 | convolution fusion | flops 2147483648 | bytes 19398656 | tf_op jit(solution)/shard_map/dot_general | solution.py:154
  380.5 0.9 copy.31
  381.4 13.7 %fusion = f32[128,8192]{1,0:T(8,128)} fusion(bf16[128,1024]{0,1:T(8,128)(2,1)} %bitcast.152, bf16[1,8192,1024]{2,1,0:T(8,128)(2,1)} %all-gather.22.cloned.1.call-done), kind=kOutput, calls=%fused_computation | convolution fusion | flops 2147483648 | bytes 21233664 | tf_op jit(solution)/shard_map/dot_general | solution.py:160
  395.1 4.9 convolution_add_fusion.1
  399.9 5.4 fusion.5
  405.4 56.1 %reduce-scatter.4.cloned.1.call-done = bf16[1024,128]{0,1:T(8,128)(2,1)} async-done(((bf16[8192,128]{0,1:T(8,128)(2,1)}), bf16[1024,128]{0,1:T(8,128)(2,1)}) %reduce-scatter.4.cloned.1.call-update) | async-done | bytes 262160 | tf_op jit(solution)/shard_map/reduce_scatter | solution.py:170
  461.5 1.1 fusion.49
  462.6 13.3 %psum.30 = f32[128]{0:T(128)S(1)} all-reduce(f32[128]{0:T(128)S(1)} %fusion.49), channel_id=1, replica_groups=mesh['section'=8,'fsdp'=4,'tensor'=8] {'tensor'}, use_global_device_ids=true, to_apply=%region_9.10 | all-reduce | flops 128 | bytes 1024 | tf_op jit(solution)/shard_map/psum | solution.py:106
  475.9 2.5 fusion.28
  478.5 3.2 convolution_convert_fusion
  481.8 73.3 %all-reduce.3.cloned.1.call-done = bf16[128,1024]{1,0:T(8,128)(2,1)} async-done(((bf16[128,1024]{1,0:T(8,128)(2,1)}), bf16[128,1024]{1,0:T(8,128)(2,1)}) %all-reduce.3.cloned.1.call-update) | async-done | bytes 262160 | tf_op jit(solution)/shard_map/psum | solution.py:182
  555.1 6.0 collective-permute-start.1
  561.1 7.7 %collective-permute-done.1 = bf16[128,1024]{1,0:T(8,128)(2,1)S(1)} collective-permute-done((bf16[128,1024]{1,0:T(8,128)(2,1)}, bf16[128,1024]{1,0:T(8,128)(2,1)S(1)}, u32[]{:S(2)}, u32[]{:S(2)}) %collective-permute-start.1) | collective-permute-done | bytes 262176 | tf_op jit(solution)/shard_map/ppermute | solution.py:17
  568.8 2.0 convolution_convert_fusion.1
  571.1 0.9 copy.34
  572.5 1.2 fusion.32
  573.7 20.1 %reduce-scatter.8.cloned.1.call-done = bf16[256,1024]{1,0:T(8,128)(2,1)} async-done(((bf16[1024,1024]{1,0:T(8,128)(2,1)}), bf16[256,1024]{1,0:T(8,128)(2,1)}) %reduce-scatter.8.cloned.1.call-update) | async-done | bytes 524304 | tf_op jit(solution)/shard_map/reduce_scatter | solution.py:110
  593.8 2.1 bitcast_convert_fusion
  596.0 32.3 %reduce-scatter.6.cloned.1.call-done = bf16[256,1024]{1,0:T(8,128)(2,1)} async-done(((bf16[1024,1024]{1,0:T(8,128)(2,1)}), bf16[256,1024]{1,0:T(8,128)(2,1)}) %reduce-scatter.6.cloned.1.call-update) | async-done | bytes 524304 | tf_op jit(solution)/shard_map/reduce_scatter | solution.py:110
  628.3 2.1 bitcast_convert_fusion.1
  (94 shorter events, 12.3 us)
Async XLA Ops:
  7.2 39.6 %copy-start = (bf16[1,128,1024]{2,1,0:T(8,128)(2,1)S(1)}, bf16[1,128,1024]{2,1,0:T(8,128)(2,1)}, u32[]{:S(2)}) copy-start(bf16[1,128,1024]{2,1,0:T(8,128)(2,1)} %param.8) | copy-start | bytes 786436
  7.2 39.6 %all-gather.14.cloned.1.call-start = ((), (), s32[]{:S(2)}) async-start(), calls=%async_computation.8 | async-start | bytes 2621440 | tf_op jit(solution)/shard_map/all_gather | solution.py:135
  7.9 88.7 %all-gather.16.cloned.1.call-start = ((), (), s32[]{:S(2)}) async-start(), calls=%async_computation.9 | async-start | bytes 2621440 | tf_op jit(solution)/shard_map/all_gather | solution.py:136
  8.7 115.0 %all-gather.20.cloned.1.call-start = ((), (), s32[]{:S(2)}) async-start(), calls=%async_computation.11 | async-start | bytes 2621440 | tf_op jit(solution)/shard_map/all_gather | solution.py:151
  9.4 166.3 %all-gather.12.cloned.1.call-start = ((), (), s32[]{:S(2)}) async-start(), calls=%async_computation.3 | async-start | bytes 2359296 | tf_op jit(solution)/shard_map/all_gather | solution.py:146
  87.7 13.6 %collective-permute-start = (bf16[128,1024]{1,0:T(8,128)(2,1)S(1)}, bf16[128,1024]{1,0:T(8,128)(2,1)S(1)}, u32[]{:S(2)}, u32[]{:S(2)}) collective-permute-start(bf16[128,1024]{1,0:T(8,128)(2,1)S(1)} %all-reduce.4), channel_id=1, source_target_pairs={{0,32},{32,64},{64,96},{96,128},{128,160},{160,192},{192,224},{224... | collective-permute-start | bytes 786440 | tf_op jit(solution)/shard_map/ppermute | solution.py:17
  101.2 19.6 %copy-start.5 = (bf16[128,1024]{1,0:T(8,128)(2,1)}, bf16[128,1024]{1,0:T(8,128)(2,1)S(1)}, u32[]{:S(2)}) copy-start(bf16[128,1024]{1,0:T(8,128)(2,1)S(1)} %collective-permute-done) | copy-start | bytes 786436
  120.2 90.2 %all-gather.18.cloned.1.call-start = ((), (), s32[]{:S(2)}) async-start(), calls=%async_computation.10 | async-start | bytes 2621440 | tf_op jit(solution)/shard_map/all_gather | solution.py:152
  120.8 1.0 copy-start.7
  120.8 1.7 copy-start.24
  120.9 247.9 %all-gather.22.cloned.1.call-start = ((), (), s32[]{:S(2)}) async-start(), calls=%async_computation.12 | async-start | bytes 20971520 | tf_op jit(solution)/shard_map/all_gather | solution.py:150
  121.4 340.1 %reduce-scatter.4.cloned.1.call-start = ((), (), s32[]{:S(2)}) async-start(), calls=%async_computation.4 | async-start | bytes 2359296 | tf_op jit(solution)/shard_map/reduce_scatter | solution.py:170
  122.5 56.5 %copy-start.17 = (f32[64]{0:T(128)}, f32[64]{0:T(128)S(1)}, u32[]{:S(2)}) copy-start(f32[64]{0:T(128)S(1)} %multiply_exponential_fusion) | copy-start | bytes 772
  122.7 56.4 %copy-start.19 = (f32[128]{0:T(128)}, f32[128]{0:T(128)S(1)}, u32[]{:S(2)}) copy-start(f32[128]{0:T(128)S(1)} %subtract_convert_fusion.2) | copy-start | bytes 1540
  175.7 34.7 %copy-start.1 = (bf16[128,8192]{1,0:T(8,128)(2,1)S(1)}, bf16[128,8192]{1,0:T(8,128)(2,1)}, u32[]{:S(2)}) copy-start(bf16[128,8192]{1,0:T(8,128)(2,1)} %all-gather.12.cloned.1.call-done) | copy-start | bytes 6291460
  377.2 1.0 copy-start.6
  377.2 1.0 copy-start.15
  378.4 0.9 copy-start.18
  378.4 0.9 copy-start.20
  381.4 13.7 %copy-start.2 = (bf16[1,8192,128]{2,1,0:T(8,128)(2,1)S(1)}, bf16[1,8192,128]{2,1,0:T(8,128)(2,1)}, u32[]{:S(2)}) copy-start(bf16[1,8192,128]{2,1,0:T(8,128)(2,1)} %all-gather.20.cloned.1.call-done) | copy-start | bytes 6291460
  381.4 13.7 %copy-start.11 = (bf16[128,1,64]{0,2,1:T(8,128)(2,1)S(1)}, bf16[128,1,64]{0,2,1:T(8,128)(2,1)}, u32[]{:S(2)}) copy-start(bf16[128,1,64]{0,2,1:T(8,128)(2,1)} %get-tuple-element.19) | copy-start | bytes 49156
  395.1 4.9 copy-start.10
  395.1 4.9 copy-start.14
  405.3 70.6 %copy-start.4 = (bf16[1,1024,1024]{2,1,0:T(8,128)(2,1)S(1)}, bf16[1,1024,1024]{2,1,0:T(8,128)(2,1)}, u32[]{:S(2)}) copy-start(bf16[1,1024,1024]{2,1,0:T(8,128)(2,1)} %all-gather.16.cloned.1.call-done) | copy-start | bytes 6291460
  405.3 70.6 %copy-start.22 = (f32[128]{0:T(128)S(1)}, f32[128]{0:T(128)}, u32[]{:S(2)}) copy-start(f32[128]{0:T(128)} %copy-done.21) | copy-start | bytes 1540
  405.3 70.6 %copy-start.23 = (f32[128]{0:T(128)S(1)}, f32[128]{0:T(128)}, u32[]{:S(2)}) copy-start(f32[128]{0:T(128)} %get-tuple-element.24) | copy-start | bytes 1540
  405.4 149.7 %all-reduce.3.cloned.1.call-start = ((), (), s32[]{:S(2)}) async-start(), calls=%async_computation.5 | async-start | bytes 524288 | tf_op jit(solution)/shard_map/psum | solution.py:182
  478.5 115.4 %reduce-scatter.8.cloned.1.call-start = ((), (), s32[]{:S(2)}) async-start(), calls=%async_computation.7 | async-start | bytes 2621440 | tf_op jit(solution)/shard_map/reduce_scatter | solution.py:110
  481.8 89.1 %copy-start.16 = (bf16[128,128,1]{1,0,2:T(8,128)(2,1)S(1)}, bf16[128,128,1]{1,0,2:T(8,128)(2,1)}, u32[]{:S(2)}) copy-start(bf16[128,128,1]{1,0,2:T(8,128)(2,1)} %fusion.44) | copy-start | bytes 98308
  481.8 146.5 %reduce-scatter.6.cloned.1.call-start = ((), (), s32[]{:S(2)}) async-start(), calls=%async_computation.6 | async-start | bytes 2621440 | tf_op jit(solution)/shard_map/reduce_scatter | solution.py:110
  555.1 13.7 %collective-permute-start.1 = (bf16[128,1024]{1,0:T(8,128)(2,1)}, bf16[128,1024]{1,0:T(8,128)(2,1)S(1)}, u32[]{:S(2)}, u32[]{:S(2)}) collective-permute-start(bf16[128,1024]{1,0:T(8,128)(2,1)} %all-reduce.3.cloned.1.call-done), channel_id=1, source_target_pairs={{0,224},{32,0},{64,32},{96,64},{128,96},{160,128},{192,160},{224,1... | collective-permute-start | bytes 786440 | tf_op jit(solution)/shard_map/ppermute | solution.py:17
  570.9 1.7 copy-start.3
  (5 other events, 3.8 us)
Sparse Core Ops, SparseCore 0:
  9.8 36.9 all-gather.13
  48.6 33.3 all-gather.15
  83.8 33.3 all-gather.19
  120.4 55.3 all-gather.11
  177.4 32.9 all-gather.17
  212.1 156.6 all-gather.21
  405.5 55.9 reduce-scatter.3
  478.6 76.4 all-reduce.2
  557.7 36.1 reduce-scatter.7
  596.2 31.9 reduce-scatter.5
where the time goes:
time: 638 us; the launch traced here: 637 us
  waiting for transfers between devices  473 us (74%)
  blocking collectives  67.2 us (11%)
  matrix products  53.3 us (8%)
  starting transfers between devices  15.5 us (2%)
  between operations  14.5 us (2%)
  other arithmetic  10.2 us (2%)
    all_gather x1, waiting for transfers between devices, body(): lax.all_gather(query_weight[0], 'fsdp', axis=0, tiled=True)  155 us
    psum x1, waiting for transfers between devices, body(): code_grad_sent = lax.psum(code_grad_partial.astype(jnp.bfloat16), 'tensor')  73.3 us
    reduce_scatter x1, waiting for transfers between devices, body(): lax.psum_scatter(total.astype(jnp.bfloat16), 'tensor', scatter_dimension=...  56.1 us
    reduce_scatter x2, waiting for transfers between devices, token_sum(): lax.psum_scatter(lax.dot_general(left, right, (((0,), (0,)), ((), ())), p...  52.5 us
    all_gather x1, waiting for transfers between devices, body(): normed_full = lax.all_gather(normed, 'tensor', axis=1, tiled=True)  52 us
    psum x1, blocking collectives, body(): code_sent = lax.psum(code_partial, 'tensor').astype(jnp.bfloat16)  38.5 us
    all_gather x1, waiting for transfers between devices, body(): lax.all_gather(encoder_weight[0], 'fsdp', axis=0, tiled=True)  37.3 us
    all_gather x1, waiting for transfers between devices, body(): lax.all_gather(value_weight[0], 'fsdp', axis=0, tiled=True)  30.6 us
  transfers between devices with their start and end apart: 12, of which 10 were waited for; matrix products, arithmetic and copies ran while one was open for 4% of the time, Pallas kernels for 0%

commit v1 on v0

--- a/solution.py
+++ b/solution.py
@@ -179,7 +179,9 @@
     code_grad_partial = lax.dot_general(
         decoded_grad, decoder_rows, contract_last, preferred_element_type=jnp.float32
     )
-    code_grad_sent = lax.psum(code_grad_partial.astype(jnp.bfloat16), "tensor")
+    block = code_grad_partial.astype(jnp.bfloat16)
+    terms = lax.all_gather(block, "tensor")
+    code_grad_sent = jnp.sum(terms, axis=0)
     code_grad = passed_along(code_grad_sent, "section", -1)
     encoder_grad = token_sum(code_grad, residual)
     hidden_grad = jnp.dot(code_grad, encoder_rows, preferred_element_type=jnp.float32).astype(

time: 638 us -> 614 us (0.962)
  waiting for transfers between devices: 473 us -> 451 us
    psum x1 -> x0, waiting for transfers between devices: 73.3 us -> none  [body(): code_grad_sent = lax.psum(code_grad_partial.astype(jnp.bfloat16), 'tensor')]
    all_gather x0 -> x1, waiting for transfers between devices: none -> 53.5 us  [body(): terms = lax.all_gather(block, 'tensor')]
where the time goes in v1:
time: 614 us; the launch traced here: 613 us
  waiting for transfers between devices  451 us (73%)
  blocking collectives  67.2 us (11%)
  matrix products  53.3 us (9%)
  between operations  14.5 us (2%)
  other arithmetic  12.2 us (2%)
  starting transfers between devices  11.1 us (2%)
    all_gather x1, waiting for transfers between devices, body(): lax.all_gather(query_weight[0], 'fsdp', axis=0, tiled=True)  155 us
    reduce_scatter x1, waiting for transfers between devices, body(): lax.psum_scatter(total.astype(jnp.bfloat16), 'tensor', scatter_dimension=...  56.1 us
    all_gather x1, waiting for transfers between devices, body(): terms = lax.all_gather(block, 'tensor')  53.5 us
    all_gather x1, waiting for transfers between devices, body(): normed_full = lax.all_gather(normed, 'tensor', axis=1, tiled=True)  52 us
    reduce_scatter x2, waiting for transfers between devices, token_sum(): lax.psum_scatter(lax.dot_general(left, right, (((0,), (0,)), ((), ())), p...  50.3 us
    psum x1, blocking collectives, body(): code_sent = lax.psum(code_partial, 'tensor').astype(jnp.bfloat16)  38.5 us
    all_gather x1, waiting for transfers between devices, body(): lax.all_gather(encoder_weight[0], 'fsdp', axis=0, tiled=True)  37.3 us
    all_gather x1, waiting for transfers between devices, body(): lax.all_gather(value_weight[0], 'fsdp', axis=0, tiled=True)  30.6 us
  transfers between devices with their start and end apart: 12, of which 10 were waited for; matrix products, arithmetic and copies ran while one was open for 4% of the time, Pallas kernels for 0%

profile of v1, /device:TPU:1, one launch (start us, length us, event | category | flops | bytes accessed | tf_op | source)
XLA Modules:
  0.0 613.4 jit_solution(14641273075411690784)
XLA Ops:
  9.4 37.3 %all-gather.16.cloned.1.call-done = bf16[1,1024,1024]{2,1,0:T(8,128)(2,1)} async-done(((bf16[1,256,1024]{2,1,0:T(8,128)(2,1)}), bf16[1,1024,1024]{2,1,0:T(8,128)(2,1)}) %all-gather.16.cloned.1.call-update) | async-done | bytes 2097168 | tf_op jit(solution)/shard_map/all_gather | solution.py:135
  46.8 2.4 fusion.18
  49.2 38.5 %all-reduce.1 = bf16[128,1024]{1,0:T(8,128)(2,1)S(1)} all-reduce(f32[128,1024]{1,0:T(8,128)S(1)} %fusion.18), channel_id=1, replica_groups=mesh['section'=8,'fsdp'=4,'tensor'=8] {'tensor'}, use_global_device_ids=true, to_apply=%region_0.0 | all-reduce | flops 131072 | bytes 786432 | tf_op jit(solution)/shard_map/psum | solution.py:141
  87.7 8.9 %collective-permute-start = (bf16[128,1024]{1,0:T(8,128)(2,1)S(1)}, bf16[128,1024]{1,0:T(8,128)(2,1)S(1)}, u32[]{:S(2)}, u32[]{:S(2)}) collective-permute-start(bf16[128,1024]{1,0:T(8,128)(2,1)S(1)} %all-reduce.1), channel_id=1, source_target_pairs={{0,32},{32,64},{64,96},{96,128},{128,160},{160,192},{192,224},{224... | collective-permute-start | bytes 786440 | tf_op jit(solution)/shard_map/ppermute | solution.py:17
  96.6 4.6 collective-permute-done
  101.2 2.2 multiply_reduce_fusion.1
  103.5 15.4 %psum.22 = f32[128]{0:T(128)S(1)} all-reduce(f32[128]{0:T(128)S(1)} %get-tuple-element.26), channel_id=1, replica_groups=mesh['section'=8,'fsdp'=4,'tensor'=8] {'tensor'}, use_global_device_ids=true, to_apply=%region_2.0 | all-reduce | flops 128 | bytes 1024 | tf_op jit(solution)/shard_map/psum | solution.py:106
  123.7 52.0 %all-gather.14.cloned.1.call-done = bf16[128,8192]{1,0:T(8,128)(2,1)} async-done(((bf16[128,1024]{1,0:T(8,128)(2,1)}), bf16[128,8192]{1,0:T(8,128)(2,1)}) %all-gather.14.cloned.1.call-update) | async-done | bytes 2097168 | tf_op jit(solution)/shard_map/all_gather | solution.py:146
  175.7 3.3 fusion.35
  179.8 30.6 %all-gather.20.cloned.1.call-done = bf16[1,8192,128]{2,1,0:T(8,128)(2,1)} async-done(((bf16[1,2048,128]{2,1,0:T(8,128)(2,1)}), bf16[1,8192,128]{2,1,0:T(8,128)(2,1)}) %all-gather.20.cloned.1.call-update) | async-done | bytes 2097168 | tf_op jit(solution)/shard_map/all_gather | solution.py:152
  210.4 2.9 fusion.44
  213.3 155.4 %all-gather.24.cloned.1.call-done = bf16[1,8192,1024]{2,1,0:T(8,128)(2,1)} async-done(((bf16[1,2048,1024]{2,1,0:T(8,128)(2,1)}), bf16[1,8192,1024]{2,1,0:T(8,128)(2,1)}) %all-gather.24.cloned.1.call-update) | async-done | bytes 16777232 | tf_op jit(solution)/shard_map/all_gather | solution.py:150
  368.7 8.1 %fusion.22 = f32[16,8,8,128]{3,1,2,0:T(8,128)S(1)} fusion(bf16[128,8192]{1,0:T(8,128)(2,1)S(1)} %copy-done.1, bf16[1,8192,1024]{2,1,0:T(8,128)(2,1)} %all-gather.24.cloned.1.call-done), kind=kOutput, calls=%fused_computation.29 | convolution fusion | flops 2147483648 | bytes 19398656 | tf_op jit(solution)/shard_map/dot_general | solution.py:154
  381.4 13.7 %fusion = f32[128,8192]{1,0:T(8,128)} fusion(bf16[128,1024]{0,1:T(8,128)(2,1)} %bitcast.154, bf16[1,8192,1024]{2,1,0:T(8,128)(2,1)} %all-gather.24.cloned.1.call-done), kind=kOutput, calls=%fused_computation | convolution fusion | flops 2147483648 | bytes 21233664 | tf_op jit(solution)/shard_map/dot_general | solution.py:160
  395.1 4.9 convolution_add_fusion.1
  399.9 5.4 fusion.5
  405.4 56.1 %reduce-scatter.4.cloned.1.call-done = bf16[1024,128]{0,1:T(8,128)(2,1)} async-done(((bf16[8192,128]{0,1:T(8,128)(2,1)}), bf16[1024,128]{0,1:T(8,128)(2,1)}) %reduce-scatter.4.cloned.1.call-update) | async-done | bytes 262160 | tf_op jit(solution)/shard_map/reduce_scatter | solution.py:170
  461.5 1.1 fusion.49
  462.6 13.3 %psum.23 = f32[128]{0:T(128)S(1)} all-reduce(f32[128]{0:T(128)S(1)} %fusion.49), channel_id=1, replica_groups=mesh['section'=8,'fsdp'=4,'tensor'=8] {'tensor'}, use_global_device_ids=true, to_apply=%region_9.10 | all-reduce | flops 128 | bytes 1024 | tf_op jit(solution)/shard_map/psum | solution.py:106
  475.9 2.5 fusion.28
  478.5 3.2 convolution_convert_fusion
  481.8 53.5 %all-gather.26.cloned.1.call-done = bf16[1024,1024]{1,0:T(8,128)(2,1)} async-done(((bf16[128,1024]{1,0:T(8,128)(2,1)}), bf16[1024,1024]{1,0:T(8,128)(2,1)}) %all-gather.26.cloned.1.call-update) | async-done | bytes 2097168 | tf_op jit(solution)/shard_map/all_gather | solution.py:183
  535.3 2.0 reduce_sum.62
  537.3 1.5 collective-permute-start.1
  538.9 8.1 %collective-permute-done.1 = bf16[128,1024]{1,0:T(8,128)(2,1)S(1)} collective-permute-done((bf16[128,1024]{1,0:T(8,128)(2,1)S(1)}, bf16[128,1024]{1,0:T(8,128)(2,1)S(1)}, u32[]{:S(2)}, u32[]{:S(2)}) %collective-permute-start.1) | collective-permute-done | bytes 262176 | tf_op jit(solution)/shard_map/ppermute | solution.py:17
  547.0 2.0 convolution_convert_fusion.1
  549.3 0.9 copy.34
  550.8 1.2 fusion.32
  552.0 18.0 %reduce-scatter.8.cloned.1.call-done = bf16[256,1024]{1,0:T(8,128)(2,1)} async-done(((bf16[1024,1024]{1,0:T(8,128)(2,1)}), bf16[256,1024]{1,0:T(8,128)(2,1)}) %reduce-scatter.8.cloned.1.call-update) | async-done | bytes 524304 | tf_op jit(solution)/shard_map/reduce_scatter | solution.py:110
  570.0 2.1 bitcast_convert_fusion
  572.1 32.3 %reduce-scatter.6.cloned.1.call-done = bf16[256,1024]{1,0:T(8,128)(2,1)} async-done(((bf16[1024,1024]{1,0:T(8,128)(2,1)}), bf16[256,1024]{1,0:T(8,128)(2,1)}) %reduce-scatter.6.cloned.1.call-update) | async-done | bytes 524304 | tf_op jit(solution)/shard_map/reduce_scatter | solution.py:110
  604.4 2.1 bitcast_convert_fusion.1
  (95 shorter events, 13.3 us)
Async XLA Ops:
  7.2 39.6 %copy-start = (bf16[1,128,1024]{2,1,0:T(8,128)(2,1)S(1)}, bf16[1,128,1024]{2,1,0:T(8,128)(2,1)}, u32[]{:S(2)}) copy-start(bf16[1,128,1024]{2,1,0:T(8,128)(2,1)} %param.8) | copy-start | bytes 786436
  7.2 39.6 %all-gather.16.cloned.1.call-start = ((), (), s32[]{:S(2)}) async-start(), calls=%async_computation.7 | async-start | bytes 2621440 | tf_op jit(solution)/shard_map/all_gather | solution.py:135
  7.9 88.7 %all-gather.18.cloned.1.call-start = ((), (), s32[]{:S(2)}) async-start(), calls=%async_computation.8 | async-start | bytes 2621440 | tf_op jit(solution)/shard_map/all_gather | solution.py:136
  8.7 115.0 %all-gather.22.cloned.1.call-start = ((), (), s32[]{:S(2)}) async-start(), calls=%async_computation.10 | async-start | bytes 2621440 | tf_op jit(solution)/shard_map/all_gather | solution.py:151
  9.4 166.3 %all-gather.14.cloned.1.call-start = ((), (), s32[]{:S(2)}) async-start(), calls=%async_computation.3 | async-start | bytes 2359296 | tf_op jit(solution)/shard_map/all_gather | solution.py:146
  87.7 13.6 %collective-permute-start = (bf16[128,1024]{1,0:T(8,128)(2,1)S(1)}, bf16[128,1024]{1,0:T(8,128)(2,1)S(1)}, u32[]{:S(2)}, u32[]{:S(2)}) collective-permute-start(bf16[128,1024]{1,0:T(8,128)(2,1)S(1)} %all-reduce.1), channel_id=1, source_target_pairs={{0,32},{32,64},{64,96},{96,128},{128,160},{160,192},{192,224},{224... | collective-permute-start | bytes 786440 | tf_op jit(solution)/shard_map/ppermute | solution.py:17
  101.2 19.6 %copy-start.5 = (bf16[128,1024]{1,0:T(8,128)(2,1)}, bf16[128,1024]{1,0:T(8,128)(2,1)S(1)}, u32[]{:S(2)}) copy-start(bf16[128,1024]{1,0:T(8,128)(2,1)S(1)} %collective-permute-done) | copy-start | bytes 786436
  120.2 90.2 %all-gather.20.cloned.1.call-start = ((), (), s32[]{:S(2)}) async-start(), calls=%async_computation.9 | async-start | bytes 2621440 | tf_op jit(solution)/shard_map/all_gather | solution.py:152
  120.8 1.0 copy-start.7
  120.8 1.7 copy-start.24
  120.9 247.9 %all-gather.24.cloned.1.call-start = ((), (), s32[]{:S(2)}) async-start(), calls=%async_computation.11 | async-start | bytes 20971520 | tf_op jit(solution)/shard_map/all_gather | solution.py:150
  121.4 340.1 %reduce-scatter.4.cloned.1.call-start = ((), (), s32[]{:S(2)}) async-start(), calls=%async_computation.4 | async-start | bytes 2359296 | tf_op jit(solution)/shard_map/reduce_scatter | solution.py:170
  122.5 56.5 %copy-start.17 = (f32[64]{0:T(128)}, f32[64]{0:T(128)S(1)}, u32[]{:S(2)}) copy-start(f32[64]{0:T(128)S(1)} %multiply_exponential_fusion) | copy-start | bytes 772
  122.7 56.4 %copy-start.19 = (f32[128]{0:T(128)}, f32[128]{0:T(128)S(1)}, u32[]{:S(2)}) copy-start(f32[128]{0:T(128)S(1)} %subtract_convert_fusion.2) | copy-start | bytes 1540
  175.7 34.7 %copy-start.1 = (bf16[128,8192]{1,0:T(8,128)(2,1)S(1)}, bf16[128,8192]{1,0:T(8,128)(2,1)}, u32[]{:S(2)}) copy-start(bf16[128,8192]{1,0:T(8,128)(2,1)} %all-gather.14.cloned.1.call-done) | copy-start | bytes 6291460
  377.2 1.0 copy-start.6
  377.2 1.0 copy-start.15
  378.4 0.9 copy-start.18
  378.4 0.9 copy-start.20
  381.4 13.7 %copy-start.2 = (bf16[1,8192,128]{2,1,0:T(8,128)(2,1)S(1)}, bf16[1,8192,128]{2,1,0:T(8,128)(2,1)}, u32[]{:S(2)}) copy-start(bf16[1,8192,128]{2,1,0:T(8,128)(2,1)} %all-gather.22.cloned.1.call-done) | copy-start | bytes 6291460
  381.4 13.7 %copy-start.11 = (bf16[128,1,64]{0,2,1:T(8,128)(2,1)S(1)}, bf16[128,1,64]{0,2,1:T(8,128)(2,1)}, u32[]{:S(2)}) copy-start(bf16[128,1,64]{0,2,1:T(8,128)(2,1)} %get-tuple-element.19) | copy-start | bytes 49156
  395.1 4.9 copy-start.10
  395.1 4.9 copy-start.14
  405.3 70.6 %copy-start.4 = (bf16[1,1024,1024]{2,1,0:T(8,128)(2,1)S(1)}, bf16[1,1024,1024]{2,1,0:T(8,128)(2,1)}, u32[]{:S(2)}) copy-start(bf16[1,1024,1024]{2,1,0:T(8,128)(2,1)} %all-gather.18.cloned.1.call-done) | copy-start | bytes 6291460
  405.3 70.6 %copy-start.22 = (f32[128]{0:T(128)S(1)}, f32[128]{0:T(128)}, u32[]{:S(2)}) copy-start(f32[128]{0:T(128)} %copy-done.21) | copy-start | bytes 1540
  405.3 70.6 %copy-start.23 = (f32[128]{0:T(128)S(1)}, f32[128]{0:T(128)}, u32[]{:S(2)}) copy-start(f32[128]{0:T(128)} %get-tuple-element.24) | copy-start | bytes 1540
  405.4 130.0 %all-gather.26.cloned.1.call-start = ((), (), s32[]{:S(2)}) async-start(), calls=%async_computation.12 | async-start | bytes 2359296 | tf_op jit(solution)/shard_map/all_gather | solution.py:183
  478.5 91.5 %reduce-scatter.8.cloned.1.call-start = ((), (), s32[]{:S(2)}) async-start(), calls=%async_computation.6 | async-start | bytes 2621440 | tf_op jit(solution)/shard_map/reduce_scatter | solution.py:110
  481.8 122.6 %reduce-scatter.6.cloned.1.call-start = ((), (), s32[]{:S(2)}) async-start(), calls=%async_computation.5 | async-start | bytes 2621440 | tf_op jit(solution)/shard_map/reduce_scatter | solution.py:110
  537.3 11.7 %copy-start.16 = (bf16[128,128,1]{1,0,2:T(8,128)(2,1)S(1)}, bf16[128,128,1]{1,0,2:T(8,128)(2,1)}, u32[]{:S(2)}) copy-start(bf16[128,128,1]{1,0,2:T(8,128)(2,1)} %fusion.44) | copy-start | bytes 98308
  537.3 9.6 %collective-permute-start.1 = (bf16[128,1024]{1,0:T(8,128)(2,1)S(1)}, bf16[128,1024]{1,0:T(8,128)(2,1)S(1)}, u32[]{:S(2)}, u32[]{:S(2)}) collective-permute-start(bf16[128,1024]{1,0:T(8,128)(2,1)S(1)} %reduce_sum.62), channel_id=1, source_target_pairs={{0,224},{32,0},{64,32},{96,64},{128,96},{160,128},{192,160},{224,1... | collective-permute-start | bytes 786440 | tf_op jit(solution)/shard_map/ppermute | solution.py:17
  549.0 1.8 copy-start.3
  (5 other events, 3.8 us)
Sparse Core Ops, SparseCore 0:
  9.8 36.9 all-gather.15
  48.6 33.3 all-gather.17
  83.8 33.3 all-gather.21
  120.4 55.3 all-gather.13
  177.4 32.9 all-gather.19
  212.1 156.6 all-gather.23
  405.5 55.9 reduce-scatter.3
  478.6 56.7 all-gather.25
  537.9 32.0 reduce-scatter.7
  572.4 31.9 reduce-scatter.5
